TPU v7x, 32 devices: a whole 2x2x4 slice. The times are simulated.
32 devices in a mesh: inp: 8 (over z, core), tm: 4 (over y, x).
Axes of the slice: x: 2, y: 2, z: 4, core: 2. Of those that a mesh axis runs over, the one named last changes fastest.
Arguments:
- samples: bfloat16 [256, 786432], P('inp', 'tm'), may hold values from -6 to 6
- tap_weights: float32 [4, 512], replicated, may hold values from -3 to 3
Outputs:
- visibilities: float32 [256, 2, 256, 256], P('tm', None, 'inp')
All inputs are finite; a program needn't handle non-finite values.
Results may differ from a plain program's by a relative error of at most 0.00081.
Values may be sent and summed in bfloat16 or wider, within the bound.
A program may use at most 128 MiB of HBM per device.

v0:
```python
import math
import jax
import jax.numpy as jnp
from jax import lax
from jax.sharding import PartitionSpec as P


def passed_along(block, axis, distance):
    devices = range(lax.axis_size(axis))
    route = [(i - distance, i) for i in devices if i - distance in devices]
    return lax.ppermute(block, axis, route)


def filter_taps(extended, weights, count):
    total = weights[0][None, None, :] * extended[:, 0:count, :].astype(jnp.float32)
    for tap in range(1, weights.shape[0]):
        total = total + weights[tap][None, None, :] * extended[:, tap : tap + count, :].astype(
            jnp.float32
        )
    return total


def per_device(samples, tap_weights):
    in_dev = samples.shape[0]
    frame = tap_weights.shape[1]
    taps = tap_weights.shape[0]
    rim = taps - 1
    spectra_dev = samples.shape[1] // frame
    frames = samples.reshape(in_dev, spectra_dev, frame)
    before = passed_along(frames[:, spectra_dev - rim :, :], "tm", 1)
    filtered = filter_taps(jnp.concatenate([before, frames], axis=1), tap_weights, spectra_dev)
    n_inp = lax.axis_size("inp")
    n_time = lax.axis_size("tm")
    ch_dev = frame // 2 // n_inp
    column = jnp.arange(frame, dtype=jnp.int32)
    remain = column % (2 * ch_dev)
    channel = column // (2 * ch_dev) * ch_dev + remain % ch_dev
    is_real = remain // ch_dev == 0
    index_n = jnp.arange(frame, dtype=jnp.int32)
    phase = index_n[:, None] * channel[None, :] % frame
    angle = phase.astype(jnp.float32) * (2.0 * math.pi / frame)
    table = jnp.where(is_real[None, :], jnp.cos(angle), -jnp.sin(angle)) * frame ** (-0.5)
    spectra = jnp.einsum(
        "isn,nj->ijs",
        filtered,
        table,
        precision=lax.Precision.HIGHEST,
        preferred_element_type=jnp.float32,
    ).astype(jnp.bfloat16)
    turned = lax.all_to_all(spectra, "inp", split_axis=1, concat_axis=0, tiled=True)
    inputs = turned.shape[0]
    turned = turned.reshape(inputs, 2, ch_dev, spectra_dev)
    real_part = jnp.einsum("ipcs,jpcs->icj", turned, turned, preferred_element_type=jnp.float32)
    imag_part = jnp.einsum(
        "ics,jcs->icj", turned[:, 1], turned[:, 0], preferred_element_type=jnp.float32
    ) - jnp.einsum("ics,jcs->icj", turned[:, 0], turned[:, 1], preferred_element_type=jnp.float32)
    mine = lax.psum_scatter(
        jnp.stack([real_part, imag_part], axis=1), "tm", scatter_dimension=0, tiled=True
    )
    return mine * (1.0 / math.sqrt(spectra_dev * n_time))


def solution(mesh):
    return jax.shard_map(
        per_device,
        mesh=mesh,
        in_specs=(P("inp", "tm"), P()),
        out_specs=P("tm", None, "inp", None),
        check_vma=False,
    )
```

profile of v0, /device:TPU:0, one launch (start us, length us, event | category | flops | bytes accessed | tf_op | source)
XLA Modules:
  0.0 655.1 jit_solution(13122239102143808897)
XLA Ops:
  6.5 0.0 reduce-scatter.2.cloned.1.call-start
  6.5 0.0 copy-start.1
  6.5 9.3 %copy.28 = bf16[4,8,384,512]{3,2,1,0:T(8,128)(2,1)S(1)} copy(bf16[4,8,384,512]{3,1,2,0:T(8,128)(2,1)} %bitcast.50) | data formatting | bytes 25165824
  15.9 0.1 slice.42
  16.0 4.9 collective-permute-start
  20.9 4.3 fusion.79
  25.2 0.0 copy-done.1
  25.2 0.0 collective-permute-done
  25.2 51.8 %convert_bitcast_fusion = bf16[32,512,384]{2,1,0:T(8,128)(2,1)S(1)} fusion(bf16[32,384,512]{2,1,0:T(8,128)(2,1)S(1)} %bitcast.49, bf16[32,3,512]{2,1,0:T(4,128)(2,1)S(1)} %collective-permute-done, f32[512]{0:T(512)S(1)} %bitcast.53, f32[512]{0:T(512)S(1)} %bitcast.54, f32[512]{0:T(512)S(1)} %bitcast.52, f32[512]{0:T(512)S(1)} %bitcast.51, ...), kind=kOutput, calls=%fused_computation.24 | convolution fusion | flops 38786826240 | bytes 26320896 | tf_op jit(solution)/shard_map/isn,nj->ijs/dot_general | solution.py:43
  77.1 32.5 %copy.16 = bf16[32,512,384]{2,0,1:T(8,128)(2,1)S(1)} copy(bf16[32,512,384]{2,1,0:T(8,128)(2,1)S(1)} %convert_bitcast_fusion) | data formatting | bytes 25165824 | tf_op jit(solution)/shard_map/convert_element_type | solution.py:49
  109.6 278.4 %all_to_all.15 = bf16[32,512,384]{2,0,1:T(8,128)(2,1)S(1)} all-to-all(bf16[32,512,384]{2,0,1:T(8,128)(2,1)S(1)} %copy.16), channel_id=1, replica_groups=mesh['inp'=8,'tm'=4] {'inp'}, dimensions={1} | all-to-all | bytes 25165824 | tf_op jit(solution)/shard_map/all_to_all | solution.py:50
  388.0 14.8 %copy.18 = bf16[8,32,64,384]{3,2,1,0:T(8,128)(2,1)S(1)} copy(bf16[8,32,64,384]{3,1,2,0:T(8,128)(2,1)S(1)} %bitcast.47) | data formatting | bytes 25165824 | tf_op jit(solution)/shard_map/all_to_all | solution.py:50
  402.8 0.0 copy-start
  402.8 4.4 copy-done
  407.2 6.4 fusion.71
  413.6 20.0 %fusion.30 = f32[256,1,32,256]{0,3,2,1:T(8,128)} fusion(bf16[256,2,32,384]{3,2,1,0:T(8,128)(2,1)} %bitcast.46), kind=kOutput, calls=%fused_computation.34 | convolution fusion | flops 3221225472 | bytes 20971520 | tf_op jit(solution)/shard_map/ipcs,jpcs->icj/dot_general | solution.py:53
  433.6 11.5 %fusion.28 = f32[32,256,256]{2,1,0:T(8,128)} fusion(bf16[256,1,32,384]{3,2,1,0:T(8,128)(2,1)} %get-tuple-element.6, bf16[256,1,32,384]{3,2,1,0:T(8,128)(2,1)} %get-tuple-element.5), kind=kOutput, calls=%fused_computation.32 | convolution fusion | flops 1610612736 | bytes 20971520 | tf_op jit(solution)/shard_map/ics,jcs->icj/dot_general | solution.py:56
  445.2 14.1 %subtract_bitcast_fusion = f32[256,1,32,256]{0,3,2,1:T(8,128)} fusion(f32[32,256,256]{2,1,0:T(8,128)} %fusion.28, bf16[256,1,32,384]{3,2,1,0:T(8,128)(2,1)} %get-tuple-element.5, bf16[256,1,32,384]{3,2,1,0:T(8,128)(2,1)} %get-tuple-element.6), kind=kOutput, calls=%fused_computation.29 | convolution fusion | flops 1612709888 | bytes 29360128 | tf_op jit(solution)/shard_map/ics,jcs->icj/dot_general | solution.py:54
  459.2 11.5 %pad_maximum_fusion = f32[256,2,32,256]{0,3,2,1:T(8,128)} fusion(f32[256,1,32,256]{0,3,2,1:T(8,128)} %subtract_bitcast_fusion, f32[256,1,32,256]{0,3,2,1:T(8,128)} %fusion.30), kind=kLoop, calls=%fused_computation.14 | loop fusion | flops 4194304 | bytes 33554432 | tf_op jit(solution)/shard_map/stack | solution.py:58
  470.8 19.9 %copy.23 = f32[256,2,32,256]{3,2,1,0:T(8,128)} copy(f32[256,2,32,256]{0,3,2,1:T(8,128)} %pad_maximum_fusion) | data formatting | bytes 33554432 | tf_op jit(solution)/shard_map/stack | solution.py:58
  490.7 0.0 reduce-scatter.2.cloned.1.call-update
  490.7 152.1 %reduce-scatter.2.cloned.1.call-done = f32[64,2,32,256]{3,2,1,0:T(8,128)} async-done(((f32[256,2,32,256]{3,2,1,0:T(8,128)}), f32[64,2,32,256]{3,2,1,0:T(8,128)}) %reduce-scatter.2.cloned.1.call-update) | async-done | bytes 4194320 | tf_op jit(solution)/shard_map/reduce_scatter | solution.py:57
  642.9 5.1 broadcast_multiply_fusion
  (3 shorter events, 0.0 us)
Async XLA Ops:
  6.5 636.3 %reduce-scatter.2.cloned.1.call-start = ((), (), s32[]{:S(2)}) async-start(), calls=%async_computation.2 | async-start | bytes 20971520 | tf_op jit(solution)/shard_map/reduce_scatter | solution.py:57
  6.5 18.7 %copy-start.1 = (f32[4,512]{1,0:T(4,128)S(1)}, f32[4,512]{1,0:T(4,128)}, u32[]{:S(2)}) copy-start(f32[4,512]{1,0:T(4,128)} %param.3) | copy-start | bytes 24580
  16.0 9.3 %collective-permute-start = (bf16[32,3,512]{2,1,0:T(4,128)(2,1)S(1)}, bf16[32,3,512]{2,1,0:T(4,128)(2,1)S(1)}, u32[]{:S(2)}, u32[]{:S(2)}) collective-permute-start(bf16[32,3,512]{2,1,0:T(4,128)(2,1)S(1)} %slice.42), channel_id=1, source_target_pairs={{0,1},{1,2},{2,3},{4,5},{5,6},{6,7},{8,9},{9,10},{10,11},{12,13},{... | collective-permute-start | bytes 294920 | tf_op jit(solution)/shard_map/ppermute | solution.py:11
  402.8 4.5 copy-start
Sparse Core Ops, SparseCore 0:
  490.8 151.9 reduce-scatter.1
where the time goes:
time: 661 us; the launch traced here: 655 us
  blocking collectives  278 us (42%)
  waiting for transfers between devices  152 us (23%)
  matrix products  97.4 us (15%)
  local copies, waits for them, and re-layouts  87.5 us (13%)
  other arithmetic  21 us (3%)
  between operations  13.7 us (2%)
    all_to_all x1, blocking collectives, per_device(): lax.all_to_all(spectra, 'inp', split_axis=1, concat_axis=0, tiled=True)  278 us
    reduce_scatter x1, waiting for transfers between devices, per_device(): lax.psum_scatter(jnp.stack([real_part, imag_part], axis=1), 'tm', scatter...  152 us
    dot_general x1, matrix products, per_device(): jnp.einsum('isn,nj->ijs', filtered, table, precision=lax.Precision.HIGHES...  51.8 us
    convert_element_type x1, local copies, waits for them, and re-layouts, per_device(): spectra = jnp.einsum('isn,nj->ijs', filtered, table, precision=lax.Precis...  32.5 us
    dot_general x1, matrix products, per_device(): jnp.einsum('ipcs,jpcs->icj', turned, turned, preferred_element_type=jnp.f...  20 us
    another operation x1, local copies, waits for them, and re-layouts, per_device(): jnp.stack([real_part, imag_part], axis=1)  19.9 us
    all_to_all x1, local copies, waits for them, and re-layouts, per_device(): lax.all_to_all(spectra, 'inp', split_axis=1, concat_axis=0, tiled=True)  14.8 us
    dot_general x1, matrix products, per_device(): jnp.einsum('ics,jcs->icj', turned[:, 1], turned[:, 0], preferred_element_...  14.1 us
  transfers between devices with their start and end apart: 2, of which 1 were waited for; matrix products, arithmetic and copies ran while one was open for 1% of the time, Pallas kernels for 0%

commit v1 on v0

--- a/solution.py
+++ b/solution.py
@@ -21,6 +21,14 @@
 
 
 def per_device(samples, tap_weights):
+
+    def _extend_leaves(xin):
+        local_next = lax.axis_size("inp")
+        passed = jnp.split(xin, local_next, axis=1)
+        tall = jnp.stack(passed)
+        local_part = lax.all_to_all(tall, "inp", 0, 0)
+        return jnp.concatenate(local_part, axis=0)
+
     in_dev = samples.shape[0]
     frame = tap_weights.shape[1]
     taps = tap_weights.shape[0]
@@ -47,7 +55,7 @@
         precision=lax.Precision.HIGHEST,
         preferred_element_type=jnp.float32,
     ).astype(jnp.bfloat16)
-    turned = lax.all_to_all(spectra, "inp", split_axis=1, concat_axis=0, tiled=True)
+    turned = _extend_leaves(spectra)
     inputs = turned.shape[0]
     turned = turned.reshape(inputs, 2, ch_dev, spectra_dev)
     real_part = jnp.einsum("ipcs,jpcs->icj", turned, turned, preferred_element_type=jnp.float32)

time: 661 us -> 616 us (0.932)
  local copies, waits for them, and re-layouts: 87.5 us -> 43.8 us
    convert_element_type x1 -> x0, local copies, waits for them, and re-layouts: 32.5 us -> none  [per_device(): spectra = jnp.einsum('isn,nj->ijs', filtered, table, precision=lax.Precis...]
    all_to_all x1 -> x0, local copies, waits for them, and re-layouts: 14.8 us -> none  [per_device(): lax.all_to_all(spectra, 'inp', split_axis=1, concat_axis=0, tiled=True)]
    unnamed x5 -> x12, local copies, waits for them, and re-layouts: 13.8 us -> 14.2 us
where the time goes in v1:
time: 616 us; the launch traced here: 610 us
  blocking collectives  279 us (45%)
  waiting for transfers between devices  152 us (25%)
  matrix products  96 us (16%)
  local copies, waits for them, and re-layouts  43.8 us (7%)
  other arithmetic  21 us (3%)
  between operations  13.8 us (2%)
    all_to_all x1, blocking collectives, _extend_leaves(): local_part = lax.all_to_all(tall, 'inp', 0, 0)  279 us
    reduce_scatter x1, waiting for transfers between devices, per_device(): lax.psum_scatter(jnp.stack([real_part, imag_part], axis=1), 'tm', scatter...  152 us
    dot_general x1, matrix products, per_device(): jnp.einsum('isn,nj->ijs', filtered, table, precision=lax.Precision.HIGHES...  51.8 us
    dot_general x1, matrix products, per_device(): jnp.einsum('ipcs,jpcs->icj', turned, turned, preferred_element_type=jnp.f...  20 us
    another operation x1, local copies, waits for them, and re-layouts, per_device(): jnp.stack([real_part, imag_part], axis=1)  19.9 us
    unnamed x12, local copies, waits for them, and re-layouts  14.2 us
    dot_general x1, matrix products, per_device(): jnp.einsum('ics,jcs->icj', turned[:, 1], turned[:, 0], preferred_element_...  14.1 us
  transfers between devices with their start and end apart: 2, of which 1 were waited for; matrix products, arithmetic and copies ran while one was open for 1% of the time, Pallas kernels for 0%

profile of v1, /device:TPU:0, one launch (start us, length us, event | category | flops | bytes accessed | tf_op | source)
XLA Modules:
  0.0 610.1 jit_solution(9926496785697509962)
XLA Ops:
  6.5 0.0 reduce-scatter.2.cloned.1.call-start
  6.5 0.0 copy-start.1
  6.5 9.3 %copy.16 = bf16[4,8,384,512]{3,2,1,0:T(8,128)(2,1)S(1)} copy(bf16[4,8,384,512]{3,1,2,0:T(8,128)(2,1)} %bitcast.78) | data formatting | bytes 25165824
  15.9 0.1 slice.42
  16.0 4.9 collective-permute-start
  20.9 4.3 fusion.87
  25.2 0.0 copy-done.1
  25.2 0.0 collective-permute-done
  25.2 51.8 %convert_bitcast_fusion = bf16[32,512,384]{2,1,0:T(8,128)(2,1)S(1)} fusion(bf16[32,384,512]{2,1,0:T(8,128)(2,1)S(1)} %bitcast.77, bf16[32,3,512]{2,1,0:T(4,128)(2,1)S(1)} %collective-permute-done, f32[512]{0:T(512)S(1)} %bitcast.81, f32[512]{0:T(512)S(1)} %bitcast.82, f32[512]{0:T(512)S(1)} %bitcast.80, f32[512]{0:T(512)S(1)} %bitcast.79, ...), kind=kOutput, calls=%fused_computation.24 | convolution fusion | flops 38786826240 | bytes 26320896 | tf_op jit(solution)/shard_map/isn,nj->ijs/dot_general | solution.py:51
  77.1 0.2 fusion.40
  77.2 0.3 fusion.39
  77.6 0.3 fusion.38
  77.9 0.3 fusion.37
  78.3 0.3 fusion.36
  78.6 0.3 fusion.35
  79.0 0.3 fusion.34
  79.3 0.3 fusion.33
  79.7 278.5 %all_to_all.5 = bf16[8,32,64,384]{3,2,1,0:T(8,128)(2,1)} all-to-all(bf16[8,32,64,384]{3,2,1,0:T(8,128)(2,1)S(1)} %fusion.33), channel_id=1, replica_groups=mesh['inp'=8,'tm'=4] {'inp'}, dimensions={0} | all-to-all | bytes 25165824 | tf_op jit(solution)/shard_map/all_to_all | solution.py:29
  358.2 20.0 %fusion.30 = f32[256,1,32,256]{0,3,2,1:T(8,128)} fusion(bf16[256,2,32,384]{3,2,1,0:T(8,128)(2,1)} %bitcast.74), kind=kOutput, calls=%fused_computation.34 | convolution fusion | flops 3221225472 | bytes 20971520 | tf_op jit(solution)/shard_map/ipcs,jpcs->icj/dot_general | solution.py:61
  378.2 9.2 %fusion.79 = (bf16[256,1,32,384]{3,2,1,0:T(8,128)(2,1)S(1)}, bf16[256,1,32,384]{3,2,1,0:T(8,128)(2,1)}) fusion(bf16[256,2,32,384]{3,2,1,0:T(8,128)(2,1)} %bitcast.75), kind=kLoop, calls=%fused_computation.102 | loop fusion | bytes 25165824 | tf_op jit(solution)/shard_map/slice | solution.py:63
  387.4 0.0 copy-start
  387.4 2.6 copy-done
  390.1 10.2 %fusion.28 = f32[32,256,256]{2,1,0:T(8,128)} fusion(bf16[256,1,32,384]{3,2,1,0:T(8,128)(2,1)} %get-tuple-element.6, bf16[256,1,32,384]{3,2,1,0:T(8,128)(2,1)S(1)} %get-tuple-element.5), kind=kOutput, calls=%fused_computation.32 | convolution fusion | flops 1610612736 | bytes 20971520 | tf_op jit(solution)/shard_map/ics,jcs->icj/dot_general | solution.py:64
  400.2 14.1 %subtract_bitcast_fusion = f32[256,1,32,256]{0,3,2,1:T(8,128)} fusion(f32[32,256,256]{2,1,0:T(8,128)} %fusion.28, bf16[256,1,32,384]{3,2,1,0:T(8,128)(2,1)} %copy-done, bf16[256,1,32,384]{3,2,1,0:T(8,128)(2,1)} %get-tuple-element.6), kind=kOutput, calls=%fused_computation.29 | convolution fusion | flops 1612709888 | bytes 29360128 | tf_op jit(solution)/shard_map/ics,jcs->icj/dot_general | solution.py:62
  414.3 11.5 %pad_maximum_fusion = f32[256,2,32,256]{0,3,2,1:T(8,128)} fusion(f32[256,1,32,256]{0,3,2,1:T(8,128)} %subtract_bitcast_fusion, f32[256,1,32,256]{0,3,2,1:T(8,128)} %fusion.30), kind=kLoop, calls=%fused_computation.14 | loop fusion | flops 4194304 | bytes 33554432 | tf_op jit(solution)/shard_map/stack | solution.py:66
  425.8 19.9 %copy.12 = f32[256,2,32,256]{3,2,1,0:T(8,128)} copy(f32[256,2,32,256]{0,3,2,1:T(8,128)} %pad_maximum_fusion) | data formatting | bytes 33554432 | tf_op jit(solution)/shard_map/stack | solution.py:66
  445.8 0.0 reduce-scatter.2.cloned.1.call-update
  445.8 152.1 %reduce-scatter.2.cloned.1.call-done = f32[64,2,32,256]{3,2,1,0:T(8,128)} async-done(((f32[256,2,32,256]{3,2,1,0:T(8,128)}), f32[64,2,32,256]{3,2,1,0:T(8,128)}) %reduce-scatter.2.cloned.1.call-update) | async-done | bytes 4194320 | tf_op jit(solution)/shard_map/reduce_scatter | solution.py:65
  597.9 5.1 broadcast_multiply_fusion
  (3 shorter events, 0.0 us)
Async XLA Ops:
  6.5 591.4 %reduce-scatter.2.cloned.1.call-start = ((), (), s32[]{:S(2)}) async-start(), calls=%async_computation.2 | async-start | bytes 20971520 | tf_op jit(solution)/shard_map/reduce_scatter | solution.py:65
  6.5 18.7 %copy-start.1 = (f32[4,512]{1,0:T(4,128)S(1)}, f32[4,512]{1,0:T(4,128)}, u32[]{:S(2)}) copy-start(f32[4,512]{1,0:T(4,128)} %param.3) | copy-start | bytes 24580
  16.0 9.3 %collective-permute-start = (bf16[32,3,512]{2,1,0:T(4,128)(2,1)S(1)}, bf16[32,3,512]{2,1,0:T(4,128)(2,1)S(1)}, u32[]{:S(2)}, u32[]{:S(2)}) collective-permute-start(bf16[32,3,512]{2,1,0:T(4,128)(2,1)S(1)} %slice.42), channel_id=1, source_target_pairs={{0,1},{1,2},{2,3},{4,5},{5,6},{6,7},{8,9},{9,10},{10,11},{12,13},{... | collective-permute-start | bytes 294920 | tf_op jit(solution)/shard_map/ppermute | solution.py:11
  387.4 2.6 copy-start
Sparse Core Ops, SparseCore 0:
  445.9 151.9 reduce-scatter.1
